TPU v7x, 512 devices: a whole 4x4x16 slice. The times are simulated.
512 devices in a mesh: seq: 16 (over x, y), tensor: 32 (over z, core).
Axes of the slice: x: 4, y: 4, z: 16, core: 2. Of those that a mesh axis runs over, the one named last changes fastest.
Arguments:
- hidden: bfloat16 [256, 2048], P('seq', 'tensor'), may hold values from -6 to 6
- router_logits: float32 [256, 8], replicated, may hold values from -6 to 6
- routes: int32 [256, 2], replicated, may hold values from 0 to 7, all different within a row
- w_query: bfloat16 [8, 2048, 2048], P(None, 'tensor', 'seq'), may hold values from -0.125 to 0.125
- w_keyval: bfloat16 [2048, 2, 2048], P('tensor', None, 'seq'), may hold values from -0.125 to 0.125
- w_output: bfloat16 [8, 2048, 2048], P(None, 'seq', 'tensor'), may hold values from -0.125 to 0.125
- k_cache: bfloat16 [4096, 64, 2048], P(('seq', 'tensor')), may hold values from -720 to 720
- v_cache: bfloat16 [4096, 64, 2048], P(('seq', 'tensor')), may hold values from -6 to 6
- lengths: int32 [64], replicated, may hold values from 1 to 4096, 104857 in all
- page_table: int32 [64, 64], replicated, may hold values from 0 to 7, as said below
- home_device: int32 [64], replicated, may hold values from 0 to 15
- accepted: int32 [64], replicated, may hold values from 1 to 4
Outputs:
- attn_out: float32 [256, 2048], P('seq', 'tensor')
- new_keys: float32 [256, 2048], P('tensor', 'seq')
- new_values: float32 [256, 2048], P('tensor', 'seq')
Inputs may be any that keep to these rules, and one draw needn't show every extreme that they name: `page_table`: for each index s of seq and t of tensor, the pages j of the requests r with r // 2 = t and (home_device[r] + j) % 16 = s have distinct values.
All inputs are finite; a program needn't handle non-finite values.
Results may differ from a plain program's by a relative error of at most 0.019.
Values may be sent and summed in bfloat16 or wider, within the bound.
A program may use at most 64 MiB of HBM per device.

v0:
```python
import math

import jax
import jax.numpy as jnp
from jax import lax
from jax.sharding import PartitionSpec as P

HD = 128
Q = 4
PAGE = 64
MAXP = 64


THETA = 10000.0
NEGATIVE = -1e30


def joined_2(part, axis, combine):
    gathered = jax.tree.map(lambda a: lax.all_gather(a, axis), part)

    def take(source):
        return jax.tree.map(lambda a: lax.dynamic_index_in_dim(a, source, 0, False), gathered)

    return lax.fori_loop(
        1, lax.axis_size(axis), lambda source, state: combine(state, take(source)), take(0)
    )


def rotate(vectors, positions):
    half_width = HD // 2
    inverse = THETA ** (-(jnp.arange(half_width, dtype=jnp.float32) * 2.0 / HD))
    angles = positions.astype(jnp.float32)[..., None] * inverse
    cosine = jnp.cos(angles)
    sine_vals = jnp.sin(angles)
    front_half = vectors[..., :half_width]
    back_half = vectors[..., half_width:]
    return jnp.concatenate(
        [front_half * cosine - back_half * sine_vals, back_half * cosine + front_half * sine_vals],
        axis=-1,
    )


def combine(earlier, later):
    top_one, sums_one, accum_one = earlier
    top_two, sums_two, accum_two = later
    top_score = jnp.maximum(top_one, top_two)
    factor_one = jnp.exp(top_one - top_score)
    factor_two = jnp.exp(top_two - top_score)
    return (
        top_score,
        sums_one * factor_one + sums_two * factor_two,
        accum_one * factor_one[..., None] + accum_two * factor_two[..., None],
    )


def per_device(
    hidden,
    router_logits,
    routes,
    w_query,
    w_keyval,
    w_output,
    k_cache,
    v_cache,
    lengths,
    page_table,
    home_device,
    accepted,
):
    seq_count = lax.axis_size("seq")
    tensor_count = lax.axis_size("tensor")
    seq_index = lax.axis_index("seq")
    tensor_index = lax.axis_index("tensor")
    tok_total = routes.shape[0]
    tok_own = tok_total // tensor_count
    req_own = tok_own // Q
    experts = w_query.shape[0]
    local_width = w_query.shape[2]
    heads_here = local_width // HD
    kv_heads = heads_here * seq_count
    scaling = 1.0 / math.sqrt(HD)
    selector = routes[:, :, None] == jnp.arange(experts, dtype=jnp.int32)[None, None, :]
    columns = lax.all_gather(hidden, "seq", axis=0, tiled=True)
    picked = selector
    query_every = jnp.einsum("nd,edh->neh", columns, w_query, preferred_element_type=jnp.float32)
    query_two = jnp.sum(jnp.where(picked[:, :, :, None], query_every[:, None, :, :], 0.0), axis=2)
    keyval = jnp.einsum("nd,dch->nch", columns, w_keyval, preferred_element_type=jnp.float32)
    summed = lax.psum(jnp.concatenate([query_two, keyval], axis=1), "tensor")
    owned = lax.dynamic_slice_in_dim(summed, tensor_index * tok_own, tok_own, 0)
    lens_own = lax.dynamic_slice_in_dim(lengths, tensor_index * req_own, req_own, 0)
    homes_own = lax.dynamic_slice_in_dim(home_device, tensor_index * req_own, req_own, 0)
    accept_own = lax.dynamic_slice_in_dim(accepted, tensor_index * req_own, req_own, 0)
    steps_own = jnp.arange(tok_own, dtype=jnp.int32) % Q
    positions = jnp.repeat(lens_own, Q) + steps_own
    queries = rotate(
        owned[:, :2].reshape(tok_own, 2, heads_here, HD), positions[:, None, None]
    ).astype(jnp.bfloat16)
    keys_rotated = rotate(owned[:, 2].reshape(tok_own, heads_here, HD), positions[:, None])
    values_raw = owned[:, 3].reshape(tok_own, heads_here, HD)
    keys_fresh = keys_rotated.astype(jnp.bfloat16)
    values_fresh = values_raw.astype(jnp.bfloat16)
    queries_all = lax.all_gather(queries, "seq", axis=2, tiled=True)
    pages_here = MAXP // seq_count
    tables_own = lax.dynamic_slice_in_dim(page_table, tensor_index * req_own, req_own, 0)
    offsets = (seq_index - homes_own) % seq_count
    logical = offsets[:, None] + seq_count * jnp.arange(pages_here, dtype=jnp.int32)[None, :]
    slots = jnp.take_along_axis(tables_own, logical, axis=1)
    key_count = pages_here * PAGE
    cache_keys = k_cache[slots].reshape(req_own, key_count, kv_heads, HD)
    cache_values = v_cache[slots].reshape(req_own, key_count, kv_heads, HD)
    key_positions = (
        logical[:, :, None] * PAGE + jnp.arange(PAGE, dtype=jnp.int32)[None, None, :]
    ).reshape(req_own, key_count)
    valid = (key_positions < lens_own[:, None])[:, None, None, None, :]
    query_blocks = queries_all.reshape(req_own, Q, 2, kv_heads, HD)
    scores = (
        jnp.einsum(
            "rqkhd,rlhd->rqkhl", query_blocks, cache_keys, preferred_element_type=jnp.float32
        )
        * scaling
    )
    scores = jnp.where(valid, scores, NEGATIVE)
    top_local = jnp.max(scores, axis=-1)
    weights = jnp.where(valid, jnp.exp(scores - top_local[..., None]), 0.0)
    sums_local = jnp.sum(weights, axis=-1)
    accum_local = jnp.einsum(
        "rqkhl,rlhd->rqkhd",
        weights.astype(jnp.bfloat16),
        cache_values,
        preferred_element_type=jnp.float32,
    )
    merged = joined_2((top_local, sums_local, accum_local), "seq", combine)
    top_cache = lax.dynamic_slice_in_dim(merged[0], seq_index * heads_here, heads_here, 3)
    sums_cache = lax.dynamic_slice_in_dim(merged[1], seq_index * heads_here, heads_here, 3)
    accum_cache = lax.dynamic_slice_in_dim(merged[2], seq_index * heads_here, heads_here, 3)
    own_queries = queries.reshape(req_own, Q, 2, heads_here, HD)
    own_keys = keys_fresh.reshape(req_own, Q, heads_here, HD)
    own_values = values_fresh.reshape(req_own, Q, heads_here, HD)
    causal = (jnp.arange(Q, dtype=jnp.int32)[:, None] >= jnp.arange(Q, dtype=jnp.int32)[None, :])[
        None, :, None, None, :
    ]
    fresh_scores = (
        jnp.einsum("rqkhd,rthd->rqkht", own_queries, own_keys, preferred_element_type=jnp.float32)
        * scaling
    )
    fresh_scores = jnp.where(causal, fresh_scores, NEGATIVE)
    top_fresh = jnp.max(fresh_scores, axis=-1)
    fresh_weights = jnp.where(causal, jnp.exp(fresh_scores - top_fresh[..., None]), 0.0)
    sums_fresh = jnp.sum(fresh_weights, axis=-1)
    accum_fresh = jnp.einsum(
        "rqkht,rthd->rqkhd",
        fresh_weights.astype(jnp.bfloat16),
        own_values,
        preferred_element_type=jnp.float32,
    )
    joined = combine((top_cache, sums_cache, accum_cache), (top_fresh, sums_fresh, accum_fresh))
    attended = (
        (joined[2] / joined[1][..., None]).astype(jnp.bfloat16).reshape(tok_own, 2, local_width)
    )
    chosen = jnp.sum(jnp.where(selector, router_logits[:, None, :], 0.0), axis=2)
    gate_probs = jax.nn.softmax(chosen, axis=1)
    picked = selector
    projected = jnp.einsum(
        "nkh,ehd->nked",
        lax.all_gather(attended, "tensor", axis=0, tiled=True),
        w_output,
        preferred_element_type=jnp.float32,
    )
    mixing = jnp.where(picked, gate_probs[:, :, None], 0.0)
    partial_out = jnp.sum(mixing[..., None] * projected, axis=(1, 2))
    out_rows = lax.psum_scatter(partial_out, "seq", scatter_dimension=0, tiled=True)
    rows_here = tok_total // seq_count
    global_rows = seq_index * rows_here + jnp.arange(rows_here, dtype=jnp.int32)
    kept_rows = global_rows % Q < jnp.take(accepted, global_rows // Q)
    attn_out = jnp.where(kept_rows[:, None], out_rows, 0.0)
    kept_own = steps_own < jnp.repeat(accept_own, Q)
    new_keys = jnp.where(kept_own[:, None], keys_rotated.reshape(tok_own, local_width), 0.0)
    new_values = jnp.where(kept_own[:, None], values_raw.reshape(tok_own, local_width), 0.0)
    return (attn_out, new_keys, new_values)


def solution(mesh):
    in_specs = (
        P("seq", "tensor"),
        P(),
        P(),
        P(None, "tensor", "seq"),
        P("tensor", None, "seq"),
        P(None, "seq", "tensor"),
        P(("seq", "tensor"), None, None),
        P(("seq", "tensor"), None, None),
        P(),
        P(),
        P(),
        P(),
    )
    out_specs = (P("seq", "tensor"), P("tensor", "seq"), P("tensor", "seq"))
    return jax.shard_map(
        per_device, mesh=mesh, in_specs=in_specs, out_specs=out_specs, check_vma=False
    )
```

profile of v0, /device:TPU:2, one launch (start us, length us, event | category | flops | bytes accessed | tf_op | source)
XLA Modules:
  0.0 500.7 jit_solution(9680683832339287307)
XLA Ops:
  7.2 26.6 %all_gather.27 = bf16[256,64]{1,0:T(8,128)(2,1)S(1)} all-gather(bf16[16,64]{1,0:T(8,128)(2,1)} %param.14), channel_id=1, replica_groups=mesh['seq'=16,'tensor'=32] {'seq'}, dimensions={0}, use_global_device_ids=true | all-gather | bytes 34816 | tf_op jit(solution)/shard_map/all_gather | solution.py:83
  33.8 1.2 fusion.39
  36.0 1.7 select_reduce_fusion
  41.1 2.0 gather_fusion.1
  43.1 2.2 copy.132
  45.3 1.7 bitcast_bitcast_fusion.1
  47.3 3.6 gather_fusion.2
  50.8 2.2 copy.133
  53.0 1.7 bitcast_bitcast_fusion
  54.9 191.5 %all-reduce.4.cloned.1.call-done = f32[256,4,128]{2,0,1:T(8,128)} async-done(((f32[256,4,128]{2,0,1:T(8,128)}), f32[256,4,128]{2,0,1:T(8,128)}) %all-reduce.4.cloned.1.call-update) | async-done | bytes 524304 | tf_op jit(solution)/shard_map/psum | solution.py:88
  247.4 23.3 %all_gather.28 = bf16[8,2,16,128]{3,0,1,2:T(8,128)(2,1)S(1)} all-gather(bf16[8,2,1,128]{3,0,1,2:T(8,128)(2,1)S(1)} %pad_maximum_fusion.1), channel_id=1, replica_groups=mesh['seq'=16,'tensor'=32] {'seq'}, dimensions={2}, use_global_device_ids=true | all-gather | bytes 69632 | tf_op jit(solution)/shard_map/all_gather | solution.py:102
  270.7 2.4 fusion.80
  275.4 1.3 dynamic-slice
  278.0 21.5 %all-gather.1 = f32[32,4,2,16]{3,1,2,0:T(4,128)S(1)} all-gather(f32[2,4,2,16]{3,1,2,0:T(4,128)S(1)} %copy.100), channel_id=3, replica_groups=mesh['seq'=16,'tensor'=32] {'seq'}, dimensions={0}, use_global_device_ids=true | all-gather | bytes 17408 | tf_op jit(solution)/shard_map/all_gather | solution.py:19
  299.4 23.0 %all-gather = f32[32,4,2,16]{3,1,2,0:T(4,128)S(1)} all-gather(f32[2,4,2,16]{3,1,2,0:T(4,128)S(1)} %copy.99), channel_id=2, replica_groups=mesh['seq'=16,'tensor'=32] {'seq'}, dimensions={0}, use_global_device_ids=true | all-gather | bytes 17408 | tf_op jit(solution)/shard_map/all_gather | solution.py:19
  324.3 8.6 %all-gather.5.cloned.1.call-done = f32[32,4,2,16,128]{4,3,2,1,0:T(8,128)} async-done(((f32[2,4,2,16,128]{4,3,2,1,0:T(8,128)}), f32[32,4,2,16,128]{4,3,2,1,0:T(8,128)}) %all-gather.5.cloned.1.call-update) | async-done | bytes 2097168 | tf_op jit(solution)/shard_map/all_gather | solution.py:19
  333.9 17.2 %while.19 = (s32[]{:T(128)}, f32[2,4,2,16]{3,2,1,0:T(2,128)S(1)}, f32[2,4,2,16]{3,2,1,0:T(2,128)S(1)}, f32[2,4,2,16,128]{4,3,2,1,0:T(8,128)S(1)}, f32[16,2,4,2,1...) while((s32[]{:T(128)}, f32[2,4,2,16]{3,2,1,0:T(2,128)S(1)}, ...), condition=%wide.region_8.9_spmd, body=%wide.region_7.8_spmd.sunk | while | flops 99845 | bytes 407703 | solution.py:24
  333.9 1.1 fusion.87
  335.1 1.1 fusion.87
  336.2 1.1 fusion.87
  337.4 1.1 fusion.87
  338.5 1.1 fusion.87
  339.7 1.1 fusion.87
  340.8 1.1 fusion.87
  344.2 1.1 fusion.87
  345.4 1.1 fusion.87
  346.5 1.1 fusion.87
  350.0 1.1 fusion.87
  351.6 31.1 %all_gather.35 = bf16[256,2,128]{2,0,1:T(8,128)(2,1)S(1)} all-gather(bf16[8,2,128]{2,0,1:T(8,128)(2,1)S(1)} %bitcast.153), channel_id=1, replica_groups=mesh['seq'=16,'tensor'=32] {'tensor'}, dimensions={0}, use_global_device_ids=true | all-gather | bytes 135168 | tf_op jit(solution)/shard_map/all_gather | solution.py:165
  383.8 1.4 bitcast_select_fusion
  385.1 107.7 %all-reduce.6.cloned.1.call-done = f32[256,64]{1,0:T(8,128)} async-done(((f32[256,64]{1,0:T(8,128)}), f32[256,64]{1,0:T(8,128)}) %all-reduce.6.cloned.1.call-update) | async-done | bytes 65552
  492.8 1.4 dynamic-slice_select_fusion
  (125 shorter events, 17.8 us)
Async XLA Ops:
  7.2 33.9 %copy-start = (bf16[8,64,2048]{2,1,0:T(8,128)(2,1)S(1)}, bf16[8,64,2048]{2,1,0:T(8,128)(2,1)}, u32[]{:S(2)}) copy-start(bf16[8,64,2048]{2,1,0:T(8,128)(2,1)} %param.20) | copy-start | bytes 6291460
  7.2 28.5 %copy-start.4 = (s32[256,2]{0,1:T(2,128)S(1)}, s32[256,2]{0,1:T(2,128)}, u32[]{:S(2)}) copy-start(s32[256,2]{0,1:T(2,128)} %param.16) | copy-start | bytes 6148
  7.2 239.2 %all-reduce.4.cloned.1.call-start = ((), (), s32[]{:S(2)}) async-start(), calls=%async_computation | async-start | bytes 1048576 | tf_op jit(solution)/shard_map/psum | solution.py:88
  35.0 2.7 copy-start.3
  35.7 3.2 copy-start.6
  35.7 3.4 copy-start.8
  38.8 294.1 %all-gather.5.cloned.1.call-start = ((), (), s32[]{:S(2)}) async-start(), calls=%async_computation.1 | async-start | bytes 2228224 | tf_op jit(solution)/shard_map/all_gather | solution.py:19
  246.4 26.7 %copy-start.2 = (bf16[2,256,16,128,1]{3,2,1,0,4:T(8,128)(2,1)S(1)}, bf16[2,256,16,128,1]{3,2,1,0,4:T(8,128)(2,1)}, u32[]{:S(2)}) copy-start(bf16[2,256,16,128,1]{3,2,1,0,4:T(8,128)(2,1)} %bitcast_bitcast_fusion) | copy-start | bytes 6291460
  273.1 1.4 copy-start.1
  273.1 2.3 copy-start.5
  274.4 218.4 %all-reduce.6.cloned.1.call-start = ((), (), s32[]{:S(2)}) async-start(), calls=%async_computation.2 | async-start | bytes 262144
  322.5 60.2 %copy-start.7 = (bf16[8,128,64]{1,2,0:T(8,128)(2,1)S(1)}, bf16[8,128,64]{1,2,0:T(8,128)(2,1)}, u32[]{:S(2)}) copy-start(bf16[8,128,64]{1,2,0:T(8,128)(2,1)} %param.19) | copy-start | bytes 393220
Sparse Core Ops, SparseCore 0:
  38.9 207.4 all-reduce.3
  274.5 58.3 all-gather.4
  383.9 108.8 all-reduce.5
where the time goes:
time: 502 us; the launch traced here: 501 us
  waiting for transfers between devices  308 us (61%)
  blocking collectives  125 us (25%)
  other arithmetic  23.9 us (5%)
  local copies, waits for them, and re-layouts  23.2 us (5%)
  between operations  14.7 us (3%)
  matrix products  5.03 us (1%)
    psum x1, waiting for transfers between devices, per_device(): summed = lax.psum(jnp.concatenate([query_two, keyval], axis=1), 'tensor')  191 us
    unnamed x4, waiting for transfers between devices  108 us
    all_gather x2, blocking collectives, joined_2(): gathered = jax.tree.map(lambda a: lax.all_gather(a, axis), part)  44.5 us
    all_gather x1, blocking collectives, per_device(): lax.all_gather(attended, 'tensor', axis=0, tiled=True)  31.1 us
    all_gather x1, blocking collectives, per_device(): columns = lax.all_gather(hidden, 'seq', axis=0, tiled=True)  26.6 us
    all_gather x1, blocking collectives, per_device(): queries_all = lax.all_gather(queries, 'seq', axis=2, tiled=True)  23.3 us
    add x15, other arithmetic, combine(): accum_one * factor_one[..., None] + accum_two * factor_two[..., None]  16.1 us
  transfers between devices with their start and end apart: 3, of which 3 were waited for; matrix products, arithmetic and copies ran while one was open for 4% of the time, Pallas kernels for 0%

commit v1 on v0

v1 whole, which is shorter than its diff:
```python
import math

import jax
import jax.numpy as jnp
from jax import lax
from jax.experimental import pallas as pl
from jax.experimental.pallas import tpu as pltpu
from jax.sharding import PartitionSpec as P

MESH = pl.DeviceIdType.MESH
THETA = 10000.0
NEGATIVE = -1e30
FLOOR = -1e29
F32 = jnp.float32
BF16 = jnp.bfloat16
HD = 128
E = 8
S = 16

def plane_hops(d):
    return min(d[0], 4 - d[0]) + min(d[1], 4 - d[1])


PLANE = sorted([(dx, dy) for dx in range(4) for dy in range(4)], key=plane_hops)
RING = sorted(range(S), key=lambda d: min(d, S - d))
REACH = S // 4
NEAR = RING[1 : 2 * REACH + 1]
HEAD_BLOCKS = (PLANE[0:4], PLANE[4:8], PLANE[8:12], PLANE[12:16])
RING_BLOCKS = (RING[0:5], RING[5:9], RING[9:13], RING[13:16])


def iota(shape, dim):
    return lax.broadcasted_iota(jnp.int32, shape, dim)


def dot_nt(a, b):
    return lax.dot_general(a, b, (((1,), (1,)), ((), ())), preferred_element_type=F32)


def dot_nn(a, b):
    return jnp.dot(a, b, preferred_element_type=F32)


def plane_peer(s, dx, dy):
    return (s // 4 + dx) % 4 * 4 + (s % 4 + dy) % 4


def take_all(ref, count, sem):
    part = ref.at[pl.ds(0, count)]
    pltpu.make_async_copy(part, part, sem).wait()


def pair_rows(a, b):
    a = a.reshape(S, 1, 8, HD)
    b = b.reshape(S, 1, 8, HD)
    return jnp.concatenate([a, b], axis=1).reshape(S, 16, HD)


def kernel(
    hid_ref,
    logits_hbm,
    routes_hbm,
    wq_ref,
    wkv_ref,
    wo_ref,
    kc_ref,
    vc_ref,
    len_hbm,
    table_hbm,
    home_hbm,
    acc_hbm,
    out_ref,
    nk_ref,
    nv_ref,
    hid_buf,
    wq_buf,
    wkv_buf,
    wo_buf,
    kbuf,
    vbuf,
    bias_buf,
    r_pair,
    g_pair,
    q_out,
    q_in,
    kv_out,
    kv_in,
    q_buf,
    p4s,
    p4r,
    att_buf,
    p6s,
    p6r,
    logits_ref,
    routes_ref,
    len_ref,
    table_ref,
    home_ref,
    acc_ref,
    local_sem,
    send_sem,
    recv_sem,
    q_sem,
    att_sem,
    w_send,
    w_recv,
    ready_sem,
):
    s = lax.axis_index("seq")
    t = lax.axis_index("tensor")
    z = t // 2
    c = t % 2
    other = 2 * z + 1 - c

    mine = s * 2 + c

    barrier = pltpu.get_barrier_semaphore()

    def greet(seq, tensor):
        pl.semaphore_signal(barrier, inc=1, device_id=(seq, tensor), device_id_type=MESH)

    for hops in range(REACH, 0, -1):
        for d in (hops, S - hops):
            greet(s, 2 * ((z + d) % S) + c)
        for dx, dy in PLANE:
            if plane_hops((dx, dy)) == hops:
                greet(plane_peer(s, dx, dy), t)
                greet(plane_peer(s, dx, dy), other)
    greet(s, other)

    loads = [
        pltpu.make_async_copy(hid_ref, hid_buf.at[mine], local_sem.at[0]),
        pltpu.make_async_copy(wq_ref, wq_buf.at[c], local_sem.at[1]),
        pltpu.make_async_copy(wkv_ref, wkv_buf.at[c], local_sem.at[2]),
        pltpu.make_async_copy(wo_ref, wo_buf.at[c], local_sem.at[3]),
        pltpu.make_async_copy(routes_hbm, routes_ref, local_sem.at[4]),
        pltpu.make_async_copy(logits_hbm, logits_ref, local_sem.at[5]),
        pltpu.make_async_copy(len_hbm, len_ref, local_sem.at[6]),
        pltpu.make_async_copy(home_hbm, home_ref, local_sem.at[7]),
        pltpu.make_async_copy(acc_hbm, acc_ref, local_sem.at[8]),
        pltpu.make_async_copy(table_hbm, table_ref, local_sem.at[9]),
        pltpu.make_async_copy(kc_ref, kbuf, local_sem.at[10]),
        pltpu.make_async_copy(vc_ref, vbuf, local_sem.at[11]),
    ]
    for load in loads:
        load.start()

    for load in loads[4:10]:
        load.wait()
    r_lane = routes_ref[...].astype(F32)
    logits = logits_ref[...]
    which = iota((E, 256), 0).astype(F32)
    c0 = jnp.sum(jnp.where(which == r_lane[0:1], logits, 0.0), axis=0, keepdims=True)
    c1 = jnp.sum(jnp.where(which == r_lane[1:2], logits, 0.0), axis=0, keepdims=True)
    cm = jnp.maximum(c0, c1)
    e0 = jnp.exp(c0 - cm)
    e1 = jnp.exp(c1 - cm)
    total = e0 + e1
    row8 = iota((8, 256), 0)
    packed = jnp.where(
        row8 == 0,
        r_lane[0:1],
        jnp.where(row8 == 1, r_lane[1:2], jnp.where(row8 == 2, e0 / total, e1 / total)),
    )
    cols = jnp.transpose(packed).reshape(S, 2, 8, 8)
    cols = jnp.where(c == 0, cols[:, 0], cols[:, 1]).reshape(S * 8, 8)
    wide = (S * 8, HD)
    r0 = jnp.broadcast_to(cols[:, 0:1], wide)
    r1 = jnp.broadcast_to(cols[:, 1:2], wide)
    g0 = jnp.broadcast_to(cols[:, 2:3], wide)
    g1 = jnp.broadcast_to(cols[:, 3:4], wide)

    r_pair[...] = pair_rows(r0, r1)
    g_pair[...] = pair_rows(g0, g1)

    row = iota((8, HD), 0)
    lane = iota((8, HD), 1)
    len0 = len_ref[2 * t]
    len1 = len_ref[2 * t + 1]
    pos = (jnp.where(row < 4, len0, len1) + row % 4).astype(F32)
    inverse = jnp.exp((lane % 64).astype(F32) * (-2.0 / HD * math.log(THETA)))
    angles = pos * inverse
    cosine = jnp.cos(angles)
    sine = jnp.sin(angles)
    sine = jnp.where(lane < HD // 2, -sine, sine)

    row_w = iota((16, 512), 0)
    lane_w = iota((16, 512), 1)
    slot_w = lane_w // 64
    limits = []
    for r, length in ((0, len0), (1, len1)):
        req = 2 * t + r
        off = (s - home_ref[req] + S) % S
        lim = jnp.zeros((16, 512), jnp.int32)
        for m in range(4):
            j = off + S * m
            left = jnp.minimum(jnp.maximum(length - 64 * j, 0), 64)
            lim = jnp.where(slot_w == table_ref[req, j], left, lim)
        limits.append(lim)
    lim = jnp.where((row_w // 4) % 2 == 0, limits[0], limits[1])
    bias_buf[...] = jnp.where(lane_w % 64 < lim, 0.0, NEGATIVE)

    loads[0].wait()
    pl.semaphore_wait(barrier, 31 + len(NEAR))

    trades = [
        pltpu.make_async_remote_copy(
            src_ref=src,
            dst_ref=dst.at[c],
            send_sem=w_send.at[n],
            recv_sem=w_recv.at[n],
            device_id=(s, other),
            device_id_type=MESH,
        )
        for n, (src, dst) in enumerate([(wq_ref, wq_buf), (wkv_ref, wkv_buf), (wo_ref, wo_buf)])
    ]

    def send_hidden(d, core):
        pltpu.make_async_remote_copy(
            src_ref=hid_buf.at[mine],
            dst_ref=hid_buf.at[mine],
            send_sem=send_sem.at[0],
            recv_sem=recv_sem.at[0],
            device_id=(plane_peer(s, d[0], d[1]), 2 * z + core),
            device_id_type=MESH,
        ).start()

    for d in PLANE[:0:-1]:
        send_hidden(d, c)
        send_hidden(d, 1 - c)
    for trade in trades:
        trade.start()
    send_hidden((0, 0), 1 - c)

    for d in (REACH, S - REACH):
        pl.semaphore_signal(
            ready_sem, inc=1, device_id=(s, 2 * ((z + d) % S) + c), device_id_type=MESH
        )

    loads[1].wait()
    loads[2].wait()
    trades[0].wait_recv()
    trades[1].wait_recv()
    pick_r = iota((HD, HD), 0)
    pick_c = iota((HD, HD), 1)
    pick = (pick_c == (pick_r % 64) * 2 + pick_r // 64).astype(F32).astype(BF16)
    kv_a = dot_nn(pick, wkv_buf[0]).astype(BF16)
    kv_b = dot_nn(pick, wkv_buf[1]).astype(BF16)
    w_k = jnp.concatenate([kv_a[:64], kv_b[:64]], axis=0)
    w_v = jnp.concatenate([kv_a[64:], kv_b[64:]], axis=0)

    take_all(hid_buf, 31, recv_sem.at[0])
    x = hid_buf[...].astype(F32).reshape(S, 2, 16, 64)
    x = jnp.where(c == 0, x[:, :, :8], x[:, :, 8:])
    lhs = jnp.concatenate([x[:, 0], x[:, 1]], axis=-1).reshape(S * 8, HD).astype(BF16)
    q0 = jnp.zeros(wide, F32)
    q1 = jnp.zeros(wide, F32)
    for e in range(E):
        w = jnp.concatenate([wq_buf[0, e], wq_buf[1, e]], axis=0)
        y = dot_nn(lhs, w)
        q0 = jnp.where(r0 == e, y, q0)
        q1 = jnp.where(r1 == e, y, q1)
    q_out[...] = pair_rows(q0, q1)

    pl.semaphore_wait(ready_sem, 2)

    def send_sums(src, dst, n):
        for d in RING[:0:-1]:
            peer = (z + d) % S
            pltpu.make_async_remote_copy(
                src_ref=src.at[peer],
                dst_ref=dst.at[z],
                send_sem=send_sem.at[n],
                recv_sem=recv_sem.at[n],
                device_id=(s, 2 * peer + c),
                device_id_type=MESH,
            ).start()
        dst[z] = src[z]

    send_sums(q_out, q_in, 1)
    key_part = dot_nn(lhs, w_k)
    value_part = dot_nn(lhs, w_v)
    kv_out[...] = pair_rows(key_part, value_part)

    take_all(q_in, S - 1, recv_sem.at[1])
    q_raw = jnp.sum(q_in[...], axis=0)
    cos2 = jnp.concatenate([cosine, cosine], axis=0)
    sin2 = jnp.concatenate([sine, sine], axis=0)
    queries = (q_raw * cos2 + pltpu.roll(q_raw, HD // 2, 1) * sin2).astype(BF16)
    q_buf[s] = queries

    for dx, dy in PLANE[:0:-1]:
        pltpu.make_async_remote_copy(
            src_ref=q_buf.at[s],
            dst_ref=q_buf.at[s],
            send_sem=send_sem.at[3],
            recv_sem=q_sem.at[PLANE.index((-dx % 4, -dy % 4))],
            device_id=(plane_peer(s, dx, dy), t),
            device_id_type=MESH,
        ).start()

    send_sums(kv_out, kv_in, 2)

    loads[10].wait()
    loads[11].wait()
    scaling = 1.0 / math.sqrt(HD)
    lane16 = iota((16, HD), 1)

    def send_partial(h):
        return pltpu.make_async_remote_copy(
            src_ref=p4s.at[h],
            dst_ref=p4r.at[s],
            send_sem=send_sem.at[4],
            recv_sem=recv_sem.at[4],
            device_id=(h, t),
            device_id_type=MESH,
        )

    for block in HEAD_BLOCKS:
        heads = [plane_peer(s, dx, dy) for dx, dy in block]
        spans = [pl.ds(pl.multiple_of(h * HD, HD), HD) for h in heads]
        for d, h in zip(block, heads):
            if d != (0, 0):
                n = PLANE.index(d)
                pltpu.make_async_copy(q_buf.at[h], q_buf.at[h], q_sem.at[n]).wait()
        bias = bias_buf[...]
        sc = [dot_nt(q_buf[h], kbuf[:, :, sp].reshape(512, HD)) for h, sp in zip(heads, spans)]
        sc = [x * scaling + bias for x in sc]
        tops = [jnp.maximum(jnp.max(x, axis=-1, keepdims=True), FLOOR) for x in sc]
        ws = [jnp.exp(x - top) for x, top in zip(sc, tops)]
        sums = [jnp.sum(w, axis=-1, keepdims=True) for w in ws]
        outs = [dot_nn(w.astype(BF16), vbuf[:, :, sp].reshape(512, HD)) for w, sp in zip(ws, spans)]
        for u, h in enumerate(heads):
            top, total = tops[u], sums[u]
            hi = top.astype(BF16).astype(F32)
            mid = (top - hi).astype(BF16).astype(F32)
            low = top - hi - mid
            s_hi = total.astype(BF16).astype(F32)
            s_low = total - s_hi
            stats = jnp.where(lane16 == 0, hi, 0.0)
            stats = jnp.where(lane16 == 1, mid, stats)
            stats = jnp.where(lane16 == 2, low, stats)
            stats = jnp.where(lane16 == 3, s_hi, stats)
            stats = jnp.where(lane16 == 4, s_low, stats)
            p4s[h, 0] = outs[u].astype(BF16)
            p4s[h, 1] = stats.astype(BF16)
        for d, h in zip(block, heads):
            if d == (0, 0):
                p4r[s] = p4s[s]
            else:
                send_partial(h).start()

    take_all(kv_in, S - 1, recv_sem.at[2])
    kv_sum = jnp.sum(kv_in[...], axis=0)
    k_raw = kv_sum[:8]
    v_raw = kv_sum[8:]
    k_rot = k_raw * cosine + pltpu.roll(k_raw, HD // 2, 1) * sine
    accept0 = acc_ref[2 * t]
    accept1 = acc_ref[2 * t + 1]
    kept = row % 4 < jnp.where(row < 4, accept0, accept1)
    nk_ref[...] = jnp.where(kept, k_rot, 0.0)
    nv_ref[...] = jnp.where(kept, v_raw, 0.0)
    zeros8 = jnp.zeros((8, HD), F32)
    k_fresh = jnp.concatenate([k_rot, zeros8], axis=0).astype(BF16)
    v_fresh = jnp.concatenate([v_raw, zeros8], axis=0).astype(BF16)
    f_tok = iota((16, 16), 0) % 8
    f_key = iota((16, 16), 1)
    causal = (f_key <= f_tok) & (f_key // 4 == f_tok // 4)
    f_scores = jnp.where(causal, dot_nt(queries, k_fresh) * scaling, NEGATIVE)
    f_top = jnp.max(f_scores, axis=-1, keepdims=True)
    f_w = jnp.exp(f_scores - f_top)
    f_sum = jnp.sum(f_w, axis=-1, keepdims=True)
    f_acc = dot_nn(f_w.astype(BF16), v_fresh)

    take_all(p4r, S - 1, recv_sem.at[4])
    er = iota((HD, 2 * HD), 0)
    ec = iota((HD, 2 * HD), 1)
    spread = jnp.where(ec < HD, er, er + 8)
    spread = ((spread < 3) | ((spread == 11) | (spread == 12))).astype(F32).astype(BF16)
    stat = dot_nn(p4r[:, 1].reshape(S * 16, HD), spread)
    tops = stat[:, :HD].reshape(S, 16, HD)
    sums = stat[:, HD:].reshape(S, 16, HD)
    top = jnp.maximum(jnp.max(tops, axis=0), f_top)
    factor = jnp.exp(tops - top[None])
    f_factor = jnp.exp(f_top - top)
    total = jnp.sum(factor * sums, axis=0) + f_factor * f_sum
    mixed = jnp.sum(factor * p4r[:, 0].astype(F32), axis=0) + f_factor * f_acc
    att_buf[z] = (mixed / total).astype(BF16)

    for d in RING[:0:-1]:
        pltpu.make_async_remote_copy(
            src_ref=att_buf.at[z],
            dst_ref=att_buf.at[z],
            send_sem=send_sem.at[5],
            recv_sem=att_sem.at[(S - d) % S],
            device_id=(s, 2 * ((z + d) % S) + c),
            device_id_type=MESH,
        ).start()
    loads[3].wait()
    trades[2].wait_recv()
    take_all(hid_buf, 31, send_sem.at[0])
    take_all(q_in, S - 1, send_sem.at[1])
    take_all(kv_in, S - 1, send_sem.at[2])
    take_all(q_buf, S - 1, send_sem.at[3])
    for trade in trades:
        trade.wait_send()

    def send_rows(to, core):
        return pltpu.make_async_remote_copy(
            src_ref=p6s.at[core, to],
            dst_ref=p6r.at[mine],
            send_sem=send_sem.at[6],
            recv_sem=recv_sem.at[6],
            device_id=(to, 2 * z + core),
            device_id_type=MESH,
        )

    for block in RING_BLOCKS:
        tos = [(z + d) % S for d in block]
        for d, to in zip(block, tos):
            if d != 0:
                pltpu.make_async_copy(att_buf.at[to], att_buf.at[to], att_sem.at[d]).wait()
        attended = jnp.concatenate([att_buf[to] for to in tos], axis=0)
        route = jnp.concatenate([r_pair[to] for to in tos], axis=0)
        gate = jnp.concatenate([g_pair[to] for to in tos], axis=0)
        chosen = jnp.zeros(route.shape, F32)
        for e in range(E):
            w = jnp.concatenate([wo_buf[0, e], wo_buf[1, e]], axis=0)
            chosen = jnp.where(route == e, dot_nt(attended, w), chosen)
        rows = (chosen * gate).reshape(len(block), 2, 8, HD)
        rows = rows[:, 0] + rows[:, 1]
        for u, to in enumerate(tos):
            p6s[0, to] = rows[u, :, :64]
            p6s[1, to] = rows[u, :, 64:]
            send_rows(to, 1 - c).start()

            @pl.when(to != s)
            def _():
                send_rows(to, c).start()

    p6r[mine] = p6s[c, s]
    take_all(p6r, 31, recv_sem.at[6])
    final = jnp.sum(p6r[...].reshape(S, 2, 8, 64), axis=0).reshape(16, 64)
    row_o = iota((16, 64), 0)
    step_lim = jnp.where(
        row_o < 8,
        jnp.where(row_o < 4, acc_ref[4 * s], acc_ref[4 * s + 1]),
        jnp.where(row_o < 12, acc_ref[4 * s + 2], acc_ref[4 * s + 3]),
    )
    out_ref[...] = jnp.where(row_o % 4 < step_lim, final, 0.0)

    take_all(p4r, S - 1, send_sem.at[4])
    take_all(att_buf, S - 1, send_sem.at[5])
    take_all(p6r, 31, send_sem.at[6])


def finish(attn_ref, keys_ref, values_ref, attn_out, keys_out, values_out, sem):
    copies = [
        pltpu.make_async_copy(attn_ref, attn_out, sem.at[0]),
        pltpu.make_async_copy(keys_ref, keys_out, sem.at[1]),
        pltpu.make_async_copy(values_ref, values_out, sem.at[2]),
    ]
    for copy in copies:
        copy.start()
    for copy in copies:
        copy.wait()


def per_device(
    hidden,
    router_logits,
    routes,
    w_query,
    w_keyval,
    w_output,
    k_cache,
    v_cache,
    lengths,
    page_table,
    home_device,
    accepted,
):
    vmem = pl.BlockSpec(memory_space=pltpu.VMEM)
    hbm = pl.BlockSpec(memory_space=pltpu.HBM)
    attn, keys, values = pl.pallas_call(
        kernel,
        out_shape=(
            jax.ShapeDtypeStruct((16, 64), F32),
            jax.ShapeDtypeStruct((8, HD), F32),
            jax.ShapeDtypeStruct((8, HD), F32),
        ),
        in_specs=[hbm] * 12,
        out_specs=(vmem, vmem, vmem),
        scratch_shapes=[
            pltpu.VMEM((32, 16, 64), BF16),
            pltpu.VMEM((2, E, 64, HD), BF16),
            pltpu.VMEM((2, HD, HD), BF16),
            pltpu.VMEM((2, E, 64, HD), BF16),
            pltpu.VMEM((8, 64, 2048), BF16),
            pltpu.VMEM((8, 64, 2048), BF16),
            pltpu.VMEM((16, 512), F32),
            pltpu.VMEM((S, 16, HD), F32),
            pltpu.VMEM((S, 16, HD), F32),
            pltpu.VMEM((S, 16, HD), F32),
            pltpu.VMEM((S, 16, HD), F32),
            pltpu.VMEM((S, 16, HD), F32),
            pltpu.VMEM((S, 16, HD), F32),
            pltpu.VMEM((S, 16, HD), BF16),
            pltpu.VMEM((S, 2, 16, HD), BF16),
            pltpu.VMEM((S, 2, 16, HD), BF16),
            pltpu.VMEM((S, 16, HD), BF16),
            pltpu.VMEM((2, S, 8, 64), F32),
            pltpu.VMEM((32, 8, 64), F32),
            pltpu.VMEM((E, 256), F32),
            pltpu.VMEM((2, 256), jnp.int32),
            pltpu.SMEM((64,), jnp.int32),
            pltpu.SMEM((64, 64), jnp.int32),
            pltpu.SMEM((64,), jnp.int32),
            pltpu.SMEM((64,), jnp.int32),
            pltpu.SemaphoreType.DMA((12,)),
            pltpu.SemaphoreType.DMA((7,)),
            pltpu.SemaphoreType.DMA((7,)),
            pltpu.SemaphoreType.DMA((S,)),
            pltpu.SemaphoreType.DMA((S,)),
            pltpu.SemaphoreType.DMA((3,)),
            pltpu.SemaphoreType.DMA((3,)),
            pltpu.SemaphoreType.REGULAR,
        ],
        compiler_params=pltpu.CompilerParams(
            collective_id=0, has_side_effects=True, vmem_limit_bytes=40 * 1024 * 1024
        ),
    )(
        *[
            pltpu.with_memory_space_constraint(a, pltpu.HBM)
            for a in (
                hidden,
                router_logits.T,
                routes.T,
                w_query,
                w_keyval.reshape(HD, HD),
                jnp.transpose(w_output, (0, 2, 1)),
                k_cache,
                v_cache,
                lengths,
                page_table,
                home_device,
                accepted,
            )
        ]
    )
    return pl.pallas_call(
        finish,
        out_shape=tuple(jax.ShapeDtypeStruct(a.shape, F32) for a in (attn, keys, values)),
        in_specs=[vmem] * 3,
        out_specs=(hbm,) * 3,
        scratch_shapes=[pltpu.SemaphoreType.DMA((3,))],
        compiler_params=pltpu.CompilerParams(vmem_limit_bytes=40 * 1024 * 1024),
    )(attn, keys, values)


def solution(mesh):
    in_specs = (
        P("seq", "tensor"),
        P(),
        P(),
        P(None, "tensor", "seq"),
        P("tensor", None, "seq"),
        P(None, "seq", "tensor"),
        P(("seq", "tensor"), None, None),
        P(("seq", "tensor"), None, None),
        P(),
        P(),
        P(),
        P(),
    )
    out_specs = (P("seq", "tensor"), P("tensor", "seq"), P("tensor", "seq"))
    return jax.shard_map(
        per_device, mesh=mesh, in_specs=in_specs, out_specs=out_specs, check_vma=False
    )
```

time: 502 us -> 51.6 us (0.10)
  the two profiles are of different devices: /device:TPU:2 before, /device:TPU:5 now
where the time goes in v1:
time: 51.6 us; the launch traced here: 51.4 us
  Pallas kernels  50.8 us (98%)
  between operations  0.64 us (1%)
    pallas_call x1, Pallas kernels, per_device(): pl.pallas_call(kernel, out_shape=(jax.ShapeDtypeStruct((16, 64), F32), ja...  50.2 us

profile of v1, /device:TPU:5, one launch (start us, length us, event | category | flops | bytes accessed | tf_op | source)
XLA Modules:
  0.0 51.4 jit_solution(15913791646711412030)
XLA Ops:
  0.6 50.2 %shard_map.139 = (f32[16,64]{1,0:T(8,128)S(1)}, f32[8,128]{1,0:T(8,128)S(1)}, f32[8,128]{1,0:T(8,128)S(1)}) custom-call(bf16[16,64]{1,0:T(8,128)(2,1)} %hid_ref.1, f32[8,256]{1,0:T(8,128)} %bitcast.6, s32[2,256]{1,0:T(2,128)} %bitcast.7, bf16[8,64,128]{2,1,0:T(8,128)(2,1)} %wq_ref.1, bf16[128,128]{1,0:T(8,128)(2,1)} %bitcast.5, bf16[8,64,128]{2,1,0:T(8,128)(2,1)} %bitcast.4, ...), custom_call_target="tpu_custom_call" | custom-call | tf_op jit(solution)/shard_map/pallas_call | solution.py:485
  50.8 0.6 %shard_map.140 = (f32[16,64]{1,0:T(8,128)}, f32[8,128]{1,0:T(8,128)}, f32[8,128]{1,0:T(8,128)}) custom-call(f32[16,64]{1,0:T(8,128)S(1)} %get-tuple-element.6.attn_ref, f32[8,128]{1,0:T(8,128)S(1)} %get-tuple-element.7.keys_ref, f32[8,128]{1,0:T(8,128)S(1)} %get-tuple-element.8.values_ref), custom_call_target="tpu_custom_call" | custom-call | tf_op jit(solution)/shard_map/pallas_call | solution.py:551
